TPU v7x, 256 devices: a whole 4x4x8 slice. The times are simulated.
256 devices in a mesh: dp: 4 (over x), tensor: 64 (over y, z, core).
Axes of the slice: x: 4, y: 4, z: 8, core: 2. Of those that a mesh axis runs over, the one named last changes fastest.
Arguments:
- tokens_in: bfloat16 [512, 4096], P('dp', 'tensor'), may hold values from -6 to 6
- out_grad: bfloat16 [512, 4096], P('dp', 'tensor'), may hold values from -6 to 6
- gate_blocks: bfloat16 [2048, 128, 128], P('tensor'), may hold values from -0.125 to 0.125
- up_blocks: bfloat16 [2048, 128, 128], P('tensor'), may hold values from -0.125 to 0.125
- down_blocks: bfloat16 [2048, 128, 128], P('tensor'), may hold values from -0.0625 to 0.0625
- gate_up_index: int32 [64, 32, 2], replicated, may hold values from 0 to 127, as said below
- down_index: int32 [64, 32, 2], replicated, may hold values from 0 to 127, as said below
Outputs:
- output: bfloat16 [512, 4096], P('dp', 'tensor')
- in_grad: bfloat16 [512, 4096], P('dp', 'tensor')
- gate_grads: bfloat16 [2048, 128, 128], P('tensor', 'dp')
- up_grads: bfloat16 [2048, 128, 128], P('tensor', 'dp')
- down_grads: bfloat16 [2048, 128, 128], P('tensor', 'dp')
Inputs may be any that keep to these rules, and one draw needn't show every extreme that they name: `gate_up_index`: Model-width blocks lie in 0 to 31, hidden-unit blocks in 0 to 127. No block is listed twice. The owner of hidden-unit block j is index j // 2 of tensor. Of one index's 32 entries at most 1 name hidden-unit blocks of any one owner, and in every draw some owner has exactly 1 entries from every index; other owners get from none up to all indices. `down_index`: Hidden-unit blocks lie in 0 to 127, model-width blocks in 0 to 31. No block is listed twice. The owner of hidden-unit block j is index j // 2 of tensor. Of one index's 32 entries at most 1 name hidden-unit blocks of any one owner, and in every draw some owner has exactly 1 entries from every index; other owners get from none up to all indices.
All inputs are finite; a program needn't handle non-finite values.
Results may differ from a plain program's by a relative error of at most 0.022.
Values may be sent and summed in bfloat16 or wider, within the bound.
A program may use at most 128 MiB of HBM per device.

v0:
```python
import jax
import jax.numpy as jnp
from jax import lax
from jax.sharding import PartitionSpec as P

FB = 128


def routing(index_list, key_col, other_col, own_count, slot_cap, my_index):
    tensor_size = index_list.shape[0]
    held_count = index_list.shape[1]
    key_blocks = index_list[:, :, key_col]
    other_idx = index_list[:, :, other_col]
    owners = key_blocks // own_count
    local_idx = key_blocks % own_count
    block_order = jnp.arange(held_count)
    before = block_order[None, :] < block_order[:, None]
    same_owner = owners[:, :, None] == owners[:, None, :]
    slot_rank = jnp.sum(jnp.logical_and(same_owner, before[None]), axis=2)
    slot_all = owners * slot_cap + slot_rank
    matches = jnp.logical_and(
        (owners == my_index)[:, :, None],
        slot_rank[:, :, None] == jnp.arange(slot_cap)[None, None, :],
    )
    is_found = jnp.any(matches, axis=1)
    recv_local = jnp.where(
        is_found, jnp.sum(jnp.where(matches, local_idx[:, :, None], 0), axis=1), -1
    )
    recv_other = jnp.sum(jnp.where(matches, other_idx[:, :, None], 0), axis=1)
    mine_slot = lax.dynamic_index_in_dim(slot_all, my_index, 0, keepdims=False)
    return (
        mine_slot,
        recv_local.reshape(tensor_size * slot_cap),
        recv_other.reshape(tensor_size * slot_cap),
    )


def per_device(tokens_in, out_grad, gate_blocks, up_blocks, down_blocks, gate_up_index, down_index):
    block_size = gate_blocks.shape[1]
    held_count = gate_blocks.shape[0]
    tok_rows = tokens_in.shape[0]
    tensor_size = lax.axis_size("tensor")
    my_index = lax.axis_index("tensor")
    blocks_f = FB
    own_count = blocks_f // tensor_size
    slot_cap = 2 * held_count // tensor_size
    slot_total = tensor_size * slot_cap
    gu_slot, gu_local, gu_other = routing(gate_up_index, 1, 0, own_count, slot_cap, my_index)
    dn_slot, dn_local, dn_other = routing(down_index, 0, 1, own_count, slot_cap, my_index)
    gu_mine = lax.dynamic_index_in_dim(gate_up_index, my_index, 0, keepdims=False)
    dn_mine = lax.dynamic_index_in_dim(down_index, my_index, 0, keepdims=False)
    own_ids = jnp.arange(own_count)[None, :]
    gu_onehot = (gu_local[:, None] == own_ids).astype(jnp.float32)
    dn_onehot = (dn_local[:, None] == own_ids).astype(jnp.float32)
    paired = jnp.concatenate([gate_blocks, up_blocks], axis=2)
    x_whole = lax.all_gather(tokens_in, "tensor", axis=1, tiled=True)
    blocks_d = x_whole.shape[1] // block_size
    x_blocks = x_whole.reshape(tok_rows, blocks_d, block_size)
    x_sel = jnp.take(x_blocks, gu_mine[:, 0], axis=1)
    partials = jnp.einsum("rnk,nkf->rnf", x_sel, paired, preferred_element_type=jnp.float32)
    outgoing = (
        jnp.zeros((tok_rows, slot_total, 2 * block_size), jnp.float32).at[:, gu_slot].set(partials)
    )
    arrived = lax.all_to_all(
        outgoing.astype(jnp.bfloat16), "tensor", split_axis=1, concat_axis=1, tiled=True
    ).astype(outgoing.dtype)
    col_sums = jnp.einsum("rsf,sl->rlf", arrived, gu_onehot, precision=lax.Precision.HIGHEST)
    gate_sum = col_sums[:, :, :block_size]
    up_sum = col_sums[:, :, block_size:]
    gate_sig = jax.nn.sigmoid(gate_sum)
    gate_act = gate_sum * gate_sig
    hidden = (gate_act * up_sum).astype(jnp.bfloat16)
    grad_whole = lax.all_gather(out_grad, "tensor", axis=1, tiled=True)
    grad_blocks = grad_whole.reshape(tok_rows, blocks_d, block_size)
    hidden_all = lax.all_gather(
        hidden.reshape(tok_rows, own_count * block_size), "tensor", axis=1, tiled=True
    )
    h_sel = jnp.take(hidden_all.reshape(tok_rows, blocks_f, block_size), dn_mine[:, 0], axis=1)
    out_parts = jnp.einsum("rnk,nkf->rnf", h_sel, down_blocks, preferred_element_type=jnp.float32)
    d_onehot = (dn_mine[:, 1][:, None] == jnp.arange(blocks_d)[None, :]).astype(jnp.float32)
    out_dense = jnp.einsum("rnf,nd->rdf", out_parts, d_onehot, precision=lax.Precision.HIGHEST)
    dy_sel = jnp.take(grad_blocks, dn_mine[:, 1], axis=1)
    hid_parts = jnp.einsum("rnf,nkf->rnk", dy_sel, down_blocks, preferred_element_type=jnp.float32)
    outgoing_h = (
        jnp.zeros((tok_rows, slot_total, block_size), jnp.float32).at[:, dn_slot].set(hid_parts)
    )
    arrived_dh = lax.all_to_all(
        outgoing_h.astype(jnp.bfloat16), "tensor", split_axis=1, concat_axis=1, tiled=True
    ).astype(outgoing_h.dtype)
    hidden_grad = jnp.einsum("rsf,sl->rlf", arrived_dh, dn_onehot, precision=lax.Precision.HIGHEST)
    down_w_grad = jnp.einsum("rnk,rnf->nkf", h_sel, dy_sel, preferred_element_type=jnp.float32)
    output = lax.psum_scatter(
        out_dense.reshape(tok_rows, blocks_d * block_size),
        "tensor",
        scatter_dimension=1,
        tiled=True,
    ).astype(jnp.bfloat16)
    gate_grad = hidden_grad * up_sum * gate_sig * (1.0 + gate_sum * (1.0 - gate_sig))
    up_grad = hidden_grad * gate_act
    both_grads = jnp.concatenate(
        [gate_grad.astype(jnp.bfloat16), up_grad.astype(jnp.bfloat16)], axis=2
    )
    back_send = jnp.take(both_grads, jnp.maximum(gu_local, 0), axis=1)
    back_send = jnp.where((gu_local >= 0)[None, :, None], back_send, jnp.zeros_like(back_send))
    returned = lax.all_to_all(back_send, "tensor", split_axis=1, concat_axis=1, tiled=True)
    gu_sel = jnp.take(returned, gu_slot, axis=1)
    gate_w_grad = jnp.einsum(
        "rnk,rnf->nkf", x_sel, gu_sel[:, :, :block_size], preferred_element_type=jnp.float32
    )
    up_w_grad = jnp.einsum(
        "rnk,rnf->nkf", x_sel, gu_sel[:, :, block_size:], preferred_element_type=jnp.float32
    )
    in_parts = jnp.einsum("rnf,nkf->rnk", gu_sel, paired, preferred_element_type=jnp.float32)
    r_onehot = (gu_mine[:, 0][:, None] == jnp.arange(blocks_d)[None, :]).astype(jnp.float32)
    in_dense = jnp.einsum("rnk,nd->rdk", in_parts, r_onehot, precision=lax.Precision.HIGHEST)
    in_grad = lax.psum_scatter(
        in_dense.reshape(tok_rows, blocks_d * block_size), "tensor", scatter_dimension=1, tiled=True
    ).astype(jnp.bfloat16)
    summed = (
        lax.psum_scatter(
            gate_w_grad.astype(jnp.bfloat16), "dp", scatter_dimension=1, tiled=True
        ).astype(jnp.float32),
        lax.psum_scatter(
            up_w_grad.astype(jnp.bfloat16), "dp", scatter_dimension=1, tiled=True
        ).astype(jnp.float32),
        lax.psum_scatter(
            down_w_grad.astype(jnp.bfloat16), "dp", scatter_dimension=1, tiled=True
        ).astype(jnp.float32),
    )
    return (
        output,
        in_grad,
        summed[0].astype(jnp.bfloat16),
        summed[1].astype(jnp.bfloat16),
        summed[2].astype(jnp.bfloat16),
    )


def solution(mesh):
    in_specs = (
        P("dp", "tensor"),
        P("dp", "tensor"),
        P("tensor", None, None),
        P("tensor", None, None),
        P("tensor", None, None),
        P(),
        P(),
    )
    out_specs = (
        P("dp", "tensor"),
        P("dp", "tensor"),
        P("tensor", "dp", None),
        P("tensor", "dp", None),
        P("tensor", "dp", None),
    )
    return jax.shard_map(
        per_device, mesh=mesh, in_specs=in_specs, out_specs=out_specs, check_vma=False
    )
```

profile of v0, /device:TPU:8, one launch (start us, length us, event | category | flops | bytes accessed | tf_op | source)
XLA Modules:
  0.0 843.3 jit_solution(729895510610050165)
XLA Ops:
  7.2 0.7 all-gather.8.cloned.1.call-update
  7.9 0.8 slice.35
  8.7 0.8 slice.31
  9.5 0.9 constant_dynamic-slice_fusion
  10.4 0.1 copy.124
  10.6 0.3 convert_reduce_fusion
  10.9 0.2 fusion.32
  11.1 0.2 fusion.31
  11.3 77.8 %all-gather.8.cloned.1.call-done = bf16[128,4096]{0,1:T(8,128)(2,1)} async-done(((bf16[128,64]{0,1:T(8,128)(2,1)}), bf16[128,4096]{0,1:T(8,128)(2,1)}) %all-gather.8.cloned.1.call-update) | async-done | bytes 1048592 | tf_op jit(solution)/shard_map/all_gather | solution.py:73
  89.1 1.6 copy.135
  90.7 1.7 gather_fusion.4
  92.4 2.1 fusion.12
  94.5 2.5 broadcast_in_dim.93
  97.0 5.4 scatter_fusion.1
  102.4 3.9 convert_element_type.53
  106.3 8.2 all-to-all-start.1
  114.5 0.0 all-gather.4.cloned.1.call-start
  114.5 0.7 all-gather.4.cloned.1.call-update
  115.2 0.1 copy.126
  115.3 1.4 constant_dynamic-update-slice_fusion.1
  116.8 1.5 constant_dynamic-update-slice_fusion
  118.3 79.2 %all-gather.4.cloned.1.call-done = bf16[128,4096]{0,1:T(8,128)(2,1)} async-done(((bf16[128,64]{0,1:T(8,128)(2,1)}), bf16[128,4096]{0,1:T(8,128)(2,1)}) %all-gather.4.cloned.1.call-update) | async-done | bytes 1048592 | tf_op jit(solution)/shard_map/all_gather | solution.py:56
  197.5 2.9 gather_fusion.3
  200.4 4.3 fusion.18
  204.8 4.2 broadcast_in_dim.88
  209.0 8.3 scatter_fusion
  217.3 6.0 convert_element_type.49
  223.3 8.2 all-to-all-start
  231.5 0.1 fusion.27
  231.6 2.8 fusion.2
  234.5 91.9 %all-to-all-done = bf16[128,64,256]{2,0,1:T(8,128)(2,1)} async-done(((bf16[128,64,256]{2,0,1:T(8,128)(2,1)}), bf16[128,64,256]{2,0,1:T(8,128)(2,1)}, u32[]{:S(2)}, u32[]{:S(2)}) %all-to-all-start) | async-done | bytes 4194336 | tf_op jit(solution)/shard_map/all_to_all | solution.py:64
  326.3 4.5 fusion
  330.9 0.1 fusion.22
  331.0 2.8 gather_fusion.1
  333.8 4.0 select_bitcast_fusion
  337.8 7.0 all-to-all-start.2
  344.8 0.7 copy.130
  345.7 106.2 %all-to-all-done.2 = bf16[128,64,256]{2,0,1:T(8,128)(2,1)} async-done(((bf16[128,64,256]{2,0,1:T(8,128)(2,1)}), bf16[128,64,256]{2,0,1:T(8,128)(2,1)}, u32[]{:S(2)}, u32[]{:S(2)}) %all-to-all-start.2) | async-done | bytes 4194336 | tf_op jit(solution)/shard_map/all_to_all | solution.py:105
  451.9 4.3 gather_fusion.2
  456.2 1.8 select_bitcast_fusion.1
  458.0 1.3 copy-done.1
  459.3 2.0 convolution_bitcast_fusion.1
  461.4 2.4 copy.138
  463.7 2.4 convolution_bitcast_fusion
  466.1 3.0 copy.144
  469.2 0.3 reduce-scatter.6.cloned.1.call-start
  469.5 6.4 copy.131
  475.9 3.0 gather_fusion
  478.9 0.5 convolution_bitcast_fusion.2
  479.4 0.5 copy-done.3
  479.9 2.4 fusion.6
  482.3 1.9 copy.143
  484.3 1.5 copy-done.2
  485.8 2.7 convolution_convert_fusion.2
  488.6 2.7 convolution_convert_fusion.1
  491.4 0.0 reduce-scatter.14.cloned.1.call-start
  491.4 3.2 convolution_convert_fusion
  494.6 112.1 %reduce-scatter.8.cloned.1.call-done = f32[128,64]{0,1:T(8,128)} async-done(((f32[128,4096]{0,1:T(8,128)}), f32[128,64]{0,1:T(8,128)}) %reduce-scatter.8.cloned.1.call-update) | async-done | bytes 32784 | tf_op jit(solution)/shard_map/reduce_scatter | solution.py:116
  606.7 1.4 convert_element_type.56
  608.1 142.1 %reduce-scatter.6.cloned.1.call-done = f32[128,64]{0,1:T(8,128)} async-done(((f32[128,4096]{0,1:T(8,128)}), f32[128,64]{0,1:T(8,128)}) %reduce-scatter.6.cloned.1.call-update) | async-done | bytes 32784 | tf_op jit(solution)/shard_map/reduce_scatter | solution.py:92
  750.2 1.4 convert_element_type.51
  751.5 26.8 %reduce-scatter.10.cloned.1.call-done = bf16[32,32,128]{2,1,0:T(8,128)(2,1)} async-done(((bf16[32,128,128]{2,1,0:T(8,128)(2,1)}), bf16[32,32,128]{2,1,0:T(8,128)(2,1)}) %reduce-scatter.10.cloned.1.call-update) | async-done | bytes 262160 | tf_op jit(solution)/shard_map/reduce_scatter | solution.py:120
  778.4 29.1 %reduce-scatter.12.cloned.1.call-done = bf16[32,32,128]{2,1,0:T(8,128)(2,1)} async-done(((bf16[32,128,128]{2,1,0:T(8,128)(2,1)}), bf16[32,32,128]{2,1,0:T(8,128)(2,1)}) %reduce-scatter.12.cloned.1.call-update) | async-done | bytes 262160 | tf_op jit(solution)/shard_map/reduce_scatter | solution.py:123
  807.5 29.0 %reduce-scatter.14.cloned.1.call-done = bf16[32,32,128]{2,1,0:T(8,128)(2,1)} async-done(((bf16[32,128,128]{2,1,0:T(8,128)(2,1)}), bf16[32,32,128]{2,1,0:T(8,128)(2,1)}) %reduce-scatter.14.cloned.1.call-update) | async-done | bytes 262160 | tf_op jit(solution)/shard_map/reduce_scatter | solution.py:126
  (43 shorter events, 0.6 us)
Async XLA Ops:
  7.2 85.3 %copy-start = (bf16[32,128,128]{2,1,0:T(8,128)(2,1)S(1)}, bf16[32,128,128]{2,1,0:T(8,128)(2,1)}, u32[]{:S(2)}) copy-start(bf16[32,128,128]{2,1,0:T(8,128)(2,1)} %param.13) | copy-start | bytes 3145732
  7.2 81.9 %all-gather.8.cloned.1.call-start = ((), (), s32[]{:S(2)}) async-start(), calls=%async_computation.11 | async-start | bytes 1064960 | tf_op jit(solution)/shard_map/all_gather | solution.py:73
  106.3 117.0 %all-to-all-start.1 = ((bf16[128,64,128]{2,0,1:T(8,128)(2,1)}), bf16[128,64,128]{2,0,1:T(8,128)(2,1)}, u32[]{:S(2)}, u32[]{:S(2)}) async-start(bf16[128,64,128]{2,0,1:T(8,128)(2,1)} %convert_element_type.53), calls=%async_computation.2 | async-start | bytes 4194304 | tf_op jit(solution)/shard_map/all_to_all | solution.py:87
  114.5 83.0 %all-gather.4.cloned.1.call-start = ((), (), s32[]{:S(2)}) async-start(), calls=%async_computation.8 | async-start | bytes 1064960 | tf_op jit(solution)/shard_map/all_gather | solution.py:56
  223.3 103.0 %all-to-all-start = ((bf16[128,64,256]{2,0,1:T(8,128)(2,1)}), bf16[128,64,256]{2,0,1:T(8,128)(2,1)}, u32[]{:S(2)}, u32[]{:S(2)}) async-start(bf16[128,64,256]{2,0,1:T(8,128)(2,1)} %convert_element_type.49), calls=%async_computation | async-start | bytes 8388608 | tf_op jit(solution)/shard_map/all_to_all | solution.py:64
  337.8 114.1 %all-to-all-start.2 = ((bf16[128,64,256]{2,0,1:T(8,128)(2,1)}), bf16[128,64,256]{2,0,1:T(8,128)(2,1)}, u32[]{:S(2)}, u32[]{:S(2)}) async-start(bf16[128,64,256]{2,0,1:T(8,128)(2,1)} %select_bitcast_fusion), calls=%async_computation.3 | async-start | bytes 8388608 | tf_op jit(solution)/shard_map/all_to_all | solution.py:105
  344.7 124.8 %all-gather.6.cloned.1.call-start = ((), (), s32[]{:S(2)}) async-start(), calls=%async_computation.9 | async-start | bytes 4259840 | tf_op jit(solution)/shard_map/all_gather | solution.py:75
  345.6 261.1 %reduce-scatter.8.cloned.1.call-start = ((), (), s32[]{:S(2)}) async-start(), calls=%async_computation.12 | async-start | bytes 2129920 | tf_op jit(solution)/shard_map/reduce_scatter | solution.py:116
  458.0 1.3 copy-start.1
  469.2 281.0 %reduce-scatter.6.cloned.1.call-start = ((), (), s32[]{:S(2)}) async-start(), calls=%async_computation.10 | async-start | bytes 2129920 | tf_op jit(solution)/shard_map/reduce_scatter | solution.py:92
  478.9 1.0 copy-start.3
  484.2 1.6 copy-start.2
  484.2 294.1 %reduce-scatter.10.cloned.1.call-start = ((), (), s32[]{:S(2)}) async-start(), calls=%async_computation.13 | async-start | bytes 1310720 | tf_op jit(solution)/shard_map/reduce_scatter | solution.py:120
  488.6 318.9 %reduce-scatter.12.cloned.1.call-start = ((), (), s32[]{:S(2)}) async-start(), calls=%async_computation.14 | async-start | bytes 1310720 | tf_op jit(solution)/shard_map/reduce_scatter | solution.py:123
  491.4 345.1 %reduce-scatter.14.cloned.1.call-start = ((), (), s32[]{:S(2)}) async-start(), calls=%async_computation.15 | async-start | bytes 1310720 | tf_op jit(solution)/shard_map/reduce_scatter | solution.py:126
Sparse Core Ops, SparseCore 0:
  10.8 78.2 all-gather.7
  118.1 79.3 all-gather.3
  348.9 99.5 all-gather.5
  469.3 137.3 reduce-scatter.7
  611.2 138.9 reduce-scatter.5
  753.1 25.1 reduce-scatter.9
  781.6 25.8 reduce-scatter.11
  810.6 25.8 reduce-scatter.13
where the time goes:
time: 845 us; the launch traced here: 843 us
  waiting for transfers between devices  696 us (82%)
  local copies, waits for them, and re-layouts  60 us (7%)
  matrix products  29.7 us (4%)
  starting transfers between devices  23.9 us (3%)
  other arithmetic  19.5 us (2%)
  between operations  14.4 us (2%)
    reduce_scatter x1, waiting for transfers between devices, per_device(): lax.psum_scatter(out_dense.reshape(tok_rows, blocks_d * block_size), 'ten...  142 us
    reduce_scatter x1, waiting for transfers between devices, per_device(): lax.psum_scatter(in_dense.reshape(tok_rows, blocks_d * block_size), 'tens...  112 us
    all_to_all x1, waiting for transfers between devices, per_device(): lax.all_to_all(back_send, 'tensor', split_axis=1, concat_axis=1, tiled=True)  106 us
    all_to_all x1, waiting for transfers between devices, per_device(): lax.all_to_all(outgoing.astype(jnp.bfloat16), 'tensor', split_axis=1, con...  91.9 us
    all_gather x1, waiting for transfers between devices, per_device(): x_whole = lax.all_gather(tokens_in, 'tensor', axis=1, tiled=True)  79.2 us
    all_gather x1, waiting for transfers between devices, per_device(): grad_whole = lax.all_gather(out_grad, 'tensor', axis=1, tiled=True)  77.8 us
    reduce_scatter x1, waiting for transfers between devices, per_device(): lax.psum_scatter(up_w_grad.astype(jnp.bfloat16), 'dp', scatter_dimension=...  29.1 us
    reduce_scatter x1, waiting for transfers between devices, per_device(): lax.psum_scatter(down_w_grad.astype(jnp.bfloat16), 'dp', scatter_dimensio...  29 us
  transfers between devices with their start and end apart: 11, of which 9 were waited for; matrix products, arithmetic and copies ran while one was open for 9% of the time, Pallas kernels for 0%

commit v1 on v0

--- a/solution.py
+++ b/solution.py
@@ -4,6 +4,13 @@
 from jax.sharding import PartitionSpec as P
 
 FB = 128
+
+
+def swapped_in(block, axis, dim):
+    peers = lax.axis_size(axis)
+    parts = jnp.stack([block for _ in range(peers)])
+    parts = lax.all_to_all(parts, axis, split_axis=0, concat_axis=0)
+    return jnp.concatenate(parts, axis=dim)
 
 
 def routing(index_list, key_col, other_col, own_count, slot_cap, my_index):
@@ -53,7 +60,7 @@
     gu_onehot = (gu_local[:, None] == own_ids).astype(jnp.float32)
     dn_onehot = (dn_local[:, None] == own_ids).astype(jnp.float32)
     paired = jnp.concatenate([gate_blocks, up_blocks], axis=2)
-    x_whole = lax.all_gather(tokens_in, "tensor", axis=1, tiled=True)
+    x_whole = swapped_in(tokens_in, "tensor", 1)
     blocks_d = x_whole.shape[1] // block_size
     x_blocks = x_whole.reshape(tok_rows, blocks_d, block_size)
     x_sel = jnp.take(x_blocks, gu_mine[:, 0], axis=1)

time: 845 us -> 787 us (0.931)
  waiting for transfers between devices: 696 us -> 624 us
  starting transfers between devices: 23.9 us -> 35.6 us
    all_gather x1 -> x0, waiting for transfers between devices: 79.2 us -> none  [per_device(): x_whole = lax.all_gather(tokens_in, 'tensor', axis=1, tiled=True)]
    all_to_all x1, waiting for transfers between devices: 0.01 us -> 18.8 us  [per_device(): lax.all_to_all(outgoing_h.astype(jnp.bfloat16), 'tensor', split_axis=1, c...]
    all_to_all x0 -> x1, starting transfers between devices: none -> 12.3 us  [swapped_in(): parts = lax.all_to_all(parts, axis, split_axis=0, concat_axis=0)]
    all_gather x1, waiting for transfers between devices: 77.8 us -> 67.6 us  [per_device(): grad_whole = lax.all_gather(out_grad, 'tensor', axis=1, tiled=True)]
  transfers between devices with their start and end apart: 11 -> 11, of which waited for: 9 -> 9; matrix products, arithmetic and copies ran while one was open for 9% -> 12% of each run, Pallas kernels for 0% -> 0%
where the time goes in v1:
time: 787 us; the launch traced here: 785 us
  waiting for transfers between devices  624 us (79%)
  local copies, waits for them, and re-layouts  61.8 us (8%)
  starting transfers between devices  35.6 us (5%)
  matrix products  29.5 us (4%)
  other arithmetic  19.3 us (2%)
  between operations  14.5 us (2%)
    reduce_scatter x1, waiting for transfers between devices, per_device(): lax.psum_scatter(out_dense.reshape(tok_rows, blocks_d * block_size), 'ten...  142 us
    reduce_scatter x1, waiting for transfers between devices, per_device(): lax.psum_scatter(in_dense.reshape(tok_rows, blocks_d * block_size), 'tens...  112 us
    all_to_all x1, waiting for transfers between devices, per_device(): lax.all_to_all(back_send, 'tensor', split_axis=1, concat_axis=1, tiled=True)  106 us
    all_to_all x1, waiting for transfers between devices, per_device(): lax.all_to_all(outgoing.astype(jnp.bfloat16), 'tensor', split_axis=1, con...  91.9 us
    all_gather x1, waiting for transfers between devices, per_device(): grad_whole = lax.all_gather(out_grad, 'tensor', axis=1, tiled=True)  67.6 us
    reduce_scatter x1, waiting for transfers between devices, per_device(): lax.psum_scatter(up_w_grad.astype(jnp.bfloat16), 'dp', scatter_dimension=...  29 us
    reduce_scatter x1, waiting for transfers between devices, per_device(): lax.psum_scatter(down_w_grad.astype(jnp.bfloat16), 'dp', scatter_dimensio...  29 us
    reduce_scatter x1, waiting for transfers between devices, per_device(): lax.psum_scatter(gate_w_grad.astype(jnp.bfloat16), 'dp', scatter_dimensio...  26.8 us
  transfers between devices with their start and end apart: 11, of which 9 were waited for; matrix products, arithmetic and copies ran while one was open for 12% of the time, Pallas kernels for 0%

profile of v1, /device:TPU:8, one launch (start us, length us, event | category | flops | bytes accessed | tf_op | source)
XLA Modules:
  0.0 785.1 jit_solution(705515270030132752)
XLA Ops:
  7.2 0.7 all-gather.5.cloned.1.call-update
  7.9 2.0 stack.2
  9.9 12.3 %all-to-all-start = ((bf16[64,128,64]{1,2,0:T(8,128)(2,1)}), bf16[64,128,64]{1,2,0:T(8,128)(2,1)}, u32[]{:S(2)}, u32[]{:S(2)}) async-start(bf16[64,128,64]{1,2,0:T(8,128)(2,1)} %stack.2), calls=%async_computation | async-start | bytes 2097152 | tf_op jit(solution)/shard_map/all_to_all | solution.py:12
  22.2 0.1 constant_dynamic-slice_fusion
  22.4 0.1 copy.136
  22.6 0.3 convert_reduce_fusion
  22.9 0.2 fusion.31
  23.2 67.6 %all-gather.5.cloned.1.call-done = bf16[128,4096]{0,1:T(8,128)(2,1)} async-done(((bf16[128,64]{0,1:T(8,128)(2,1)}), bf16[128,4096]{0,1:T(8,128)(2,1)}) %all-gather.5.cloned.1.call-update) | async-done | bytes 1048592 | tf_op jit(solution)/shard_map/all_gather | solution.py:80
  90.8 1.6 copy.147
  92.4 1.7 gather_fusion.4
  94.1 2.1 fusion.12
  96.2 2.4 broadcast_in_dim.93
  98.7 5.4 scatter_fusion.1
  104.0 3.9 convert_element_type.53
  107.9 8.2 %all-to-all-start.2 = ((bf16[128,64,128]{2,0,1:T(8,128)(2,1)}), bf16[128,64,128]{2,0,1:T(8,128)(2,1)}, u32[]{:S(2)}, u32[]{:S(2)}) async-start(bf16[128,64,128]{2,0,1:T(8,128)(2,1)} %convert_element_type.53), calls=%async_computation.3 | async-start | bytes 4194304 | tf_op jit(solution)/shard_map/all_to_all | solution.py:94
  116.1 0.1 copy.138
  116.2 1.4 constant_dynamic-update-slice_fusion.1
  117.6 1.5 constant_dynamic-update-slice_fusion
  119.2 2.3 copy.139
  121.4 2.9 gather_fusion.3
  124.4 3.9 fusion.18
  128.3 4.2 broadcast_in_dim.88
  132.5 8.3 %scatter_fusion = f32[128,64,256]{2,0,1:T(8,128)} fusion(f32[128,64,256]{2,0,1:T(8,128)} %broadcast_in_dim.88, s32[32]{0:T(128)S(1)} %fusion.51, f32[32,128,256]{2,1,0:T(8,128)} %fusion.18), kind=kCustom, calls=%fused_computation.5 | custom fusion | bytes 12583040 | tf_op jit(solution)/shard_map/scatter | solution.py:69
  140.8 6.0 convert_element_type.49
  146.8 18.8 %all-to-all-done.2 = bf16[128,64,128]{2,0,1:T(8,128)(2,1)} async-done(((bf16[128,64,128]{2,0,1:T(8,128)(2,1)}), bf16[128,64,128]{2,0,1:T(8,128)(2,1)}, u32[]{:S(2)}, u32[]{:S(2)}) %all-to-all-start.2) | async-done | bytes 2097184 | tf_op jit(solution)/shard_map/all_to_all | solution.py:94
  165.6 7.7 all-to-all-start.1
  173.3 0.1 fusion.27
  173.5 2.8 fusion.2
  176.3 91.9 %all-to-all-done.1 = bf16[128,64,256]{2,0,1:T(8,128)(2,1)} async-done(((bf16[128,64,256]{2,0,1:T(8,128)(2,1)}), bf16[128,64,256]{2,0,1:T(8,128)(2,1)}, u32[]{:S(2)}, u32[]{:S(2)}) %all-to-all-start.1) | async-done | bytes 4194336 | tf_op jit(solution)/shard_map/all_to_all | solution.py:71
  268.1 4.5 fusion
  272.7 0.1 fusion.22
  272.8 2.8 gather_fusion.1
  275.6 4.0 select_bitcast_fusion
  279.6 7.0 all-to-all-start.3
  286.5 0.0 all-gather.3.cloned.1.call-start
  286.6 0.7 copy.142
  287.3 0.0 reduce-scatter.8.cloned.1.call-start
  287.4 106.2 %all-to-all-done.3 = bf16[128,64,256]{2,0,1:T(8,128)(2,1)} async-done(((bf16[128,64,256]{2,0,1:T(8,128)(2,1)}), bf16[128,64,256]{2,0,1:T(8,128)(2,1)}, u32[]{:S(2)}, u32[]{:S(2)}) %all-to-all-start.3) | async-done | bytes 4194336 | tf_op jit(solution)/shard_map/all_to_all | solution.py:112
  393.7 4.2 gather_fusion.2
  397.9 1.8 select_bitcast_fusion.1
  399.8 1.3 copy-done.1
  401.1 2.0 convolution_bitcast_fusion.1
  403.1 2.4 copy.150
  405.5 2.4 convolution_bitcast_fusion
  407.9 3.0 copy.159
  410.9 0.3 reduce-scatter.6.cloned.1.call-start
  411.2 6.4 copy.143
  417.6 3.0 gather_fusion
  420.6 0.5 convolution_bitcast_fusion.2
  421.1 0.5 copy-done.3
  421.6 2.4 fusion.6
  424.0 1.9 copy.158
  426.0 1.5 copy-done.2
  427.5 2.8 convolution_convert_fusion.2
  430.4 2.8 convolution_convert_fusion.1
  433.2 0.0 reduce-scatter.14.cloned.1.call-start
  433.3 3.2 convolution_convert_fusion
  436.5 112.0 %reduce-scatter.8.cloned.1.call-done = f32[128,64]{0,1:T(8,128)} async-done(((f32[128,4096]{0,1:T(8,128)}), f32[128,64]{0,1:T(8,128)}) %reduce-scatter.8.cloned.1.call-update) | async-done | bytes 32784 | tf_op jit(solution)/shard_map/reduce_scatter | solution.py:123
  548.5 1.4 convert_element_type.56
  549.8 142.2 %reduce-scatter.6.cloned.1.call-done = f32[128,64]{0,1:T(8,128)} async-done(((f32[128,4096]{0,1:T(8,128)}), f32[128,64]{0,1:T(8,128)}) %reduce-scatter.6.cloned.1.call-update) | async-done | bytes 32784 | tf_op jit(solution)/shard_map/reduce_scatter | solution.py:99
  692.0 1.4 convert_element_type.51
  693.4 26.8 %reduce-scatter.10.cloned.1.call-done = bf16[32,32,128]{2,1,0:T(8,128)(2,1)} async-done(((bf16[32,128,128]{2,1,0:T(8,128)(2,1)}), bf16[32,32,128]{2,1,0:T(8,128)(2,1)}) %reduce-scatter.10.cloned.1.call-update) | async-done | bytes 262160 | tf_op jit(solution)/shard_map/reduce_scatter | solution.py:127
  720.3 29.0 %reduce-scatter.12.cloned.1.call-done = bf16[32,32,128]{2,1,0:T(8,128)(2,1)} async-done(((bf16[32,128,128]{2,1,0:T(8,128)(2,1)}), bf16[32,32,128]{2,1,0:T(8,128)(2,1)}) %reduce-scatter.12.cloned.1.call-update) | async-done | bytes 262160 | tf_op jit(solution)/shard_map/reduce_scatter | solution.py:130
  749.2 29.0 %reduce-scatter.14.cloned.1.call-done = bf16[32,32,128]{2,1,0:T(8,128)(2,1)} async-done(((bf16[32,128,128]{2,1,0:T(8,128)(2,1)}), bf16[32,32,128]{2,1,0:T(8,128)(2,1)}) %reduce-scatter.14.cloned.1.call-update) | async-done | bytes 262160 | tf_op jit(solution)/shard_map/reduce_scatter | solution.py:133
  (48 shorter events, 0.5 us)
Async XLA Ops:
  7.2 86.9 %copy-start = (bf16[32,128,128]{2,1,0:T(8,128)(2,1)S(1)}, bf16[32,128,128]{2,1,0:T(8,128)(2,1)}, u32[]{:S(2)}) copy-start(bf16[32,128,128]{2,1,0:T(8,128)(2,1)} %param.13) | copy-start | bytes 3145732
  7.2 15.0 %copy-start.4 = (s32[64,32,2]{0,2,1:T(2,128)S(1)}, s32[64,32,2]{0,2,1:T(2,128)}, u32[]{:S(2)}) copy-start(s32[64,32,2]{0,2,1:T(2,128)} %param.15) | copy-start | bytes 49156
  7.2 15.0 %copy-start.5 = (s32[64,32,2]{0,2,1:T(2,128)S(1)}, s32[64,32,2]{0,2,1:T(2,128)}, u32[]{:S(2)}) copy-start(s32[64,32,2]{0,2,1:T(2,128)} %param.14) | copy-start | bytes 49156
  7.2 83.6 %all-gather.5.cloned.1.call-start = ((), (), s32[]{:S(2)}) async-start(), calls=%async_computation.11 | async-start | bytes 1064960 | tf_op jit(solution)/shard_map/all_gather | solution.py:80
  9.9 98.0 %all-to-all-start = ((bf16[64,128,64]{1,2,0:T(8,128)(2,1)}), bf16[64,128,64]{1,2,0:T(8,128)(2,1)}, u32[]{:S(2)}, u32[]{:S(2)}) async-start(bf16[64,128,64]{1,2,0:T(8,128)(2,1)} %stack.2), calls=%async_computation | async-start | bytes 2097152 | tf_op jit(solution)/shard_map/all_to_all | solution.py:12
  107.9 57.6 %all-to-all-start.2 = ((bf16[128,64,128]{2,0,1:T(8,128)(2,1)}), bf16[128,64,128]{2,0,1:T(8,128)(2,1)}, u32[]{:S(2)}, u32[]{:S(2)}) async-start(bf16[128,64,128]{2,0,1:T(8,128)(2,1)} %convert_element_type.53), calls=%async_computation.3 | async-start | bytes 4194304 | tf_op jit(solution)/shard_map/all_to_all | solution.py:94
  165.6 102.6 %all-to-all-start.1 = ((bf16[128,64,256]{2,0,1:T(8,128)(2,1)}), bf16[128,64,256]{2,0,1:T(8,128)(2,1)}, u32[]{:S(2)}, u32[]{:S(2)}) async-start(bf16[128,64,256]{2,0,1:T(8,128)(2,1)} %convert_element_type.49), calls=%async_computation.1 | async-start | bytes 8388608 | tf_op jit(solution)/shard_map/all_to_all | solution.py:71
  279.6 114.1 %all-to-all-start.3 = ((bf16[128,64,256]{2,0,1:T(8,128)(2,1)}), bf16[128,64,256]{2,0,1:T(8,128)(2,1)}, u32[]{:S(2)}, u32[]{:S(2)}) async-start(bf16[128,64,256]{2,0,1:T(8,128)(2,1)} %select_bitcast_fusion), calls=%async_computation.4 | async-start | bytes 8388608 | tf_op jit(solution)/shard_map/all_to_all | solution.py:112
  286.5 124.7 %all-gather.3.cloned.1.call-start = ((), (), s32[]{:S(2)}) async-start(), calls=%async_computation.9 | async-start | bytes 4259840 | tf_op jit(solution)/shard_map/all_gather | solution.py:82
  287.3 261.1 %reduce-scatter.8.cloned.1.call-start = ((), (), s32[]{:S(2)}) async-start(), calls=%async_computation.12 | async-start | bytes 2129920 | tf_op jit(solution)/shard_map/reduce_scatter | solution.py:123
  399.8 1.3 copy-start.1
  410.9 281.1 %reduce-scatter.6.cloned.1.call-start = ((), (), s32[]{:S(2)}) async-start(), calls=%async_computation.10 | async-start | bytes 2129920 | tf_op jit(solution)/shard_map/reduce_scatter | solution.py:99
  420.6 1.0 copy-start.3
  425.9 1.6 copy-start.2
  425.9 294.3 %reduce-scatter.10.cloned.1.call-start = ((), (), s32[]{:S(2)}) async-start(), calls=%async_computation.13 | async-start | bytes 1310720 | tf_op jit(solution)/shard_map/reduce_scatter | solution.py:127
  430.4 318.9 %reduce-scatter.12.cloned.1.call-start = ((), (), s32[]{:S(2)}) async-start(), calls=%async_computation.14 | async-start | bytes 1310720 | tf_op jit(solution)/shard_map/reduce_scatter | solution.py:130
  433.2 345.0 %reduce-scatter.14.cloned.1.call-start = ((), (), s32[]{:S(2)}) async-start(), calls=%async_computation.15 | async-start | bytes 1310720 | tf_op jit(solution)/shard_map/reduce_scatter | solution.py:133
Sparse Core Ops, SparseCore 0:
  10.8 79.9 all-gather.4
  290.7 98.8 all-gather.2
  411.0 137.4 reduce-scatter.7
  552.9 139.0 reduce-scatter.5
  695.0 25.1 reduce-scatter.9
  723.4 25.8 reduce-scatter.11
  752.4 25.8 reduce-scatter.13
